TPU v7x, 32 devices: a whole 2x2x4 slice. The times are simulated.
32 devices in a mesh: blk: 4 (over y, x), inner: 8 (over z, core).
Axes of the slice: x: 2, y: 2, z: 4, core: 2. Of those that a mesh axis runs over, the one named last changes fastest.
Arguments:
- points: float32 [4096, 128], P(('blk', 'inner')), may hold values from -8 to 8
- lengthscales: float32 [128], replicated, may hold values from 6 to 24
- noise_level: float32 [1], replicated, may hold values from 1 to 10
- iterate: float32 [4096, 64], P(('blk', 'inner')), may hold values from -6 to 6
- residual: float32 [4096, 64], P(('blk', 'inner')), may hold values from -6 to 6
- direction: float32 [4096, 64], P(('blk', 'inner')), may hold values from -6 to 6
Outputs:
- new_iterate: float32 [4096, 64], P(('blk', 'inner'))
- new_residual: float32 [4096, 64], P(('blk', 'inner'))
- new_direction: float32 [4096, 64], P(('blk', 'inner'))
All inputs are finite; a program needn't handle non-finite values.
Results may differ from a plain program's by a relative error of at most 0.00014.
Values sent between devices are 32-bit elements; how exact they have to be, the bound alone decides.
A program may use at most 64 MiB of HBM per device.

v0:
```python
import jax
import jax.numpy as jnp
from jax import lax
from jax.sharding import PartitionSpec as P


def from_behind(value, axis, by):
    size = lax.axis_size(axis)
    return lax.ppermute(value, axis, [(i, (i + by) % size) for i in range(size)])


def kernel_block(left, left_sq, right, right_sq):
    products = lax.dot_general(
        left,
        right,
        (((1,), (1,)), ((), ())),
        precision=lax.Precision.HIGHEST,
        preferred_element_type=jnp.float32,
    )
    return jnp.exp(-0.5 * (left_sq[:, None] + right_sq[None, :] - 2.0 * products))


def matmul(left, right):
    return jnp.dot(left, right, precision=lax.Precision.HIGHEST, preferred_element_type=jnp.float32)


def transposed(left, right):
    return lax.dot_general(
        left,
        right,
        (((0,), (0,)), ((), ())),
        precision=lax.Precision.HIGHEST,
        preferred_element_type=jnp.float32,
    )


def chol_solve(matrix, rhs_side):
    factor = jnp.linalg.cholesky(matrix)
    return jax.scipy.linalg.cho_solve((factor, True), rhs_side)


def on_device(points, lengthscales, noise_level, iterate, residual, direction):
    scaled = points / lengthscales[None, :]
    sq_norms = jnp.sum(scaled * scaled, axis=1)
    cycle_size = lax.axis_size("blk")
    group_pts, group_dir = (
        lax.all_gather(scaled, "inner", axis=0, tiled=True),
        lax.all_gather(direction, "inner", axis=0, tiled=True),
    )
    group_sq = jnp.sum(group_pts * group_pts, axis=1)
    partial_value = jnp.zeros((group_pts.shape[0], direction.shape[1]), jnp.float32)
    halfway = cycle_size // 2
    visitor = (scaled, sq_norms, direction, jnp.zeros_like(direction))
    returned = jnp.zeros_like(direction)
    for offset in range(halfway + 1):
        if offset > 0:
            visitor = from_behind((visitor[0], visitor[1], visitor[2], visitor[3]), "blk", 1)
        kernel_tile = kernel_block(group_pts, group_sq, visitor[0], visitor[1])
        partial_value = partial_value + matmul(kernel_tile, visitor[2])
        if 1 <= offset <= halfway - 1:
            carried = visitor[3] + transposed(kernel_tile, group_dir)
            visitor = (visitor[0], visitor[1], visitor[2], carried)
            if offset == halfway - 1:
                returned = from_behind(carried, "blk", -(halfway - 1))
    owned = lax.psum_scatter(partial_value, "inner", scatter_dimension=0, tiled=True)
    image = owned + returned + noise_level[0] * direction
    local_gram = transposed(direction, image)
    local_res = transposed(residual, residual)
    gram_raw, res_gram = lax.psum((local_gram, local_res), ("blk", "inner"))
    gram_matrix = 0.5 * (gram_raw + gram_raw.T)
    step_size = chol_solve(gram_matrix, res_gram)
    new_residual = residual - matmul(image, step_size)
    new_gram = lax.psum(transposed(new_residual, new_residual), ("blk", "inner"))
    new_iterate = iterate + matmul(direction, step_size)
    correction = chol_solve(res_gram, new_gram)
    new_direction = new_residual + matmul(direction, correction)
    return (new_iterate, new_residual, new_direction)


def solution(mesh):
    return jax.shard_map(
        on_device,
        mesh=mesh,
        in_specs=(
            P(("blk", "inner"), None),
            P(),
            P(),
            P(("blk", "inner"), None),
            P(("blk", "inner"), None),
            P(("blk", "inner"), None),
        ),
        out_specs=(P(("blk", "inner"), None), P(("blk", "inner"), None), P(("blk", "inner"), None)),
        check_vma=False,
    )
```

profile of v0, /device:TPU:0, one launch (start us, length us, event | category | flops | bytes accessed | tf_op | source)
XLA Modules:
  0.0 187.7 jit_solution(3288486812774204959)
XLA Ops:
  7.2 0.0 reduce-scatter.2.cloned.1.call-start
  7.2 3.0 %collective-permute-start.6 = (f32[128,64]{0,1:T(8,128)S(1)}, f32[128,64]{0,1:T(8,128)S(1)}, u32[]{:S(2)}, u32[]{:S(2)}) collective-permute-start(f32[128,64]{0,1:T(8,128)S(1)} %broadcast_in_dim.2), channel_id=1, source_target_pairs={{0,8},{8,16},{16,24},{24,0},{1,9},{9,17},{17,25},{25,1},{2,10},{10... | collective-permute-start | bytes 98312 | tf_op jit(solution)/shard_map/ppermute | solution.py:9
  10.3 1.5 collective-permute-start.2
  11.8 0.9 multiply_reduce_fusion.1
  12.7 1.5 collective-permute-start
  14.3 0.6 collective-permute-start.1
  14.9 15.0 %all_gather.6 = f32[1024,128]{1,0:T(8,128)S(1)} all-gather(f32[128,128]{1,0:T(8,128)S(1)} %get-tuple-element.8), channel_id=1, replica_groups=mesh['blk'=4,'inner'=8] {'inner'}, dimensions={0}, use_global_device_ids=true | all-gather | bytes 589824 | tf_op jit(solution)/shard_map/all_gather | solution.py:47
  29.9 0.2 multiply_reduce_fusion
  30.1 0.6 fusion.2
  30.7 0.7 fusion.34
  31.4 1.4 collective-permute-start.3
  32.8 1.5 collective-permute-start.5
  34.3 1.5 collective-permute-start.4
  35.8 0.6 convolution_multiply_fusion.1
  36.4 0.9 convolution_add_fusion.1
  37.3 2.2 %collective-permute-done.4 = f32[128,128]{1,0:T(8,128)S(1)} collective-permute-done((f32[128,128]{1,0:T(8,128)S(1)}, f32[128,128]{1,0:T(8,128)S(1)}, u32[]{:S(2)}, u32[]{:S(2)}) %collective-permute-start.4) | collective-permute-done | bytes 65568 | tf_op jit(solution)/shard_map/ppermute | solution.py:9
  39.5 0.6 convolution_multiply_fusion
  40.1 1.6 convolution_add_fusion
  41.6 0.0 reduce-scatter.2.cloned.1.call-update
  41.7 14.3 %all_gather.7 = f32[1024,64]{0,1:T(8,128)S(1)} all-gather(f32[128,64]{0,1:T(8,128)S(1)} %copy-done), channel_id=1, replica_groups=mesh['blk'=4,'inner'=8] {'inner'}, dimensions={0}, use_global_device_ids=true | all-gather | bytes 294912 | tf_op jit(solution)/shard_map/all_gather | solution.py:48
  55.9 0.6 convolution_add_fusion.2
  56.5 0.8 collective-permute-start.7
  57.3 0.2 fusion.35
  58.2 2.3 %collective-permute-done.7 = f32[128,64]{0,1:T(8,128)S(1)} collective-permute-done((f32[128,64]{0,1:T(8,128)S(1)}, f32[128,64]{0,1:T(8,128)S(1)}, u32[]{:S(2)}, u32[]{:S(2)}) %collective-permute-start.7) | collective-permute-done | bytes 32800 | tf_op jit(solution)/shard_map/ppermute | solution.py:9
  60.5 11.5 %reduce-scatter.2.cloned.1.call-done = f32[128,64]{0,1:T(8,128)} async-done(((f32[1024,64]{0,1:T(8,128)}), f32[128,64]{0,1:T(8,128)}) %reduce-scatter.2.cloned.1.call-update) | async-done | bytes 32784 | tf_op jit(solution)/shard_map/reduce_scatter | solution.py:65
  72.0 0.9 convolution_bitcast_fusion.2
  73.0 38.3 %all-reduce = (f32[64,64]{0,1:T(8,128)S(1)}, f32[64,64]{1,0:T(8,128)S(1)}) all-reduce(f32[64,64]{0,1:T(8,128)S(1)} %fusion.35, f32[64,64]{1,0:T(8,128)S(1)} %convolution_bitcast_fusion.2), channel_id=1, replica_groups=mesh['blk'=4,'inner'=8] {'blk','inner'}, use_global_device_ids=true, to_apply=%region_6.8 | all-reduce | flops 8192 | bytes 65536 | tf_op jit(solution)/shard_map/psum | solution.py:69
  111.3 0.1 copy.10
  111.4 0.1 copy.11
  111.5 5.8 %cholesky.44 = f32[64,64]{1,0:T(8,128)S(1)} custom-call(f32[64,64]{1,0:T(8,128)S(1)} %fusion.29), custom_call_target="Cholesky" | custom-call | tf_op jit(solution)/shard_map/jit(cholesky)/cholesky | solution.py:38
  117.3 0.6 compare_reduce_fusion.1
  118.0 0.7 fusion.18
  118.6 4.9 %custom-call.8 = f32[1,64,64]{1,2,0:T(8,128)S(1)} custom-call(f32[1,64,64]{2,1,0:T(8,128)S(1)} %fusion.18), custom_call_target="InvertDiagBlocksLowerTriangular" | custom-call | tf_op jit(solution)/shard_map/jit(_cho_solve)/triangular_solve | solution.py:39
  123.5 0.1 copy.13
  123.6 0.2 fusion.27
  123.9 0.2 fusion.25
  124.1 0.6 copy-done.4
  124.6 0.9 fusion.4
  125.5 0.2 convolution_subtract_fusion
  125.8 0.2 fusion.36
  125.9 41.5 %psum.23 = f32[64,64]{1,0:T(8,128)S(1)} all-reduce(f32[64,64]{1,0:T(8,128)S(1)} %fusion.36), channel_id=1, replica_groups=mesh['blk'=4,'inner'=8] {'blk','inner'}, use_global_device_ids=true, to_apply=%region_7.10 | all-reduce | flops 4096 | bytes 32768 | tf_op jit(solution)/shard_map/psum | solution.py:73
  167.5 5.8 %cholesky.55 = f32[64,64]{1,0:T(8,128)S(1)} custom-call(f32[64,64]{1,0:T(8,128)S(1)} %fusion.24), custom_call_target="Cholesky" | custom-call | tf_op jit(solution)/shard_map/jit(cholesky)/cholesky | solution.py:38
  173.4 0.6 compare_reduce_fusion
  174.0 0.7 fusion.19
  174.7 4.9 %custom-call.9 = f32[1,64,64]{1,2,0:T(8,128)S(1)} custom-call(f32[1,64,64]{2,1,0:T(8,128)S(1)} %fusion.19), custom_call_target="InvertDiagBlocksLowerTriangular" | custom-call | tf_op jit(solution)/shard_map/jit(_cho_solve)/triangular_solve | solution.py:39
  179.6 0.3 fusion.22
  179.8 0.2 fusion.20
  180.0 0.9 fusion.3
  (23 shorter events, 0.1 us)
Async XLA Ops:
  7.2 3.1 %copy-start = (f32[128,64]{0,1:T(8,128)S(1)}, f32[128,64]{0,1:T(8,128)}, u32[]{:S(2)}) copy-start(f32[128,64]{0,1:T(8,128)} %param.14) | copy-start | bytes 98308
  7.2 4.6 %copy-start.5 = (f32[128]{0:T(128)S(1)}, f32[128]{0:T(128)}, u32[]{:S(2)}) copy-start(f32[128]{0:T(128)} %param.10) | copy-start | bytes 1540
  7.2 64.8 %reduce-scatter.2.cloned.1.call-start = ((), (), s32[]{:S(2)}) async-start(), calls=%async_computation.1 | async-start | bytes 294912 | tf_op jit(solution)/shard_map/reduce_scatter | solution.py:65
  7.2 48.7 %collective-permute-start.6 = (f32[128,64]{0,1:T(8,128)S(1)}, f32[128,64]{0,1:T(8,128)S(1)}, u32[]{:S(2)}, u32[]{:S(2)}) collective-permute-start(f32[128,64]{0,1:T(8,128)S(1)} %broadcast_in_dim.2), channel_id=1, source_target_pairs={{0,8},{8,16},{16,24},{24,0},{1,9},{9,17},{17,25},{25,1},{2,10},{10... | collective-permute-start | bytes 98312 | tf_op jit(solution)/shard_map/ppermute | solution.py:9
  10.3 22.6 %collective-permute-start.2 = (f32[128,64]{0,1:T(8,128)S(1)}, f32[128,64]{0,1:T(8,128)S(1)}, u32[]{:S(2)}, u32[]{:S(2)}) collective-permute-start(f32[128,64]{0,1:T(8,128)S(1)} %copy-done), channel_id=1, source_target_pairs={{0,8},{8,16},{16,24},{24,0},{1,9},{9,17},{17,25},{25,1},{2,10},{10... | collective-permute-start | bytes 98312 | tf_op jit(solution)/shard_map/ppermute | solution.py:9
  12.7 18.7 %collective-permute-start = (f32[128]{0:T(128)S(1)}, f32[128]{0:T(128)S(1)}, u32[]{:S(2)}, u32[]{:S(2)}) collective-permute-start(f32[128]{0:T(128)S(1)} %get-tuple-element.7), channel_id=1, source_target_pairs={{0,8},{8,16},{16,24},{24,0},{1,9},{9,17},{17,25},{25,1},{2,10},{10... | collective-permute-start | bytes 1544 | tf_op jit(solution)/shard_map/ppermute | solution.py:9
  14.3 20.1 %collective-permute-start.1 = (f32[128,128]{1,0:T(8,128)S(1)}, f32[128,128]{1,0:T(8,128)S(1)}, u32[]{:S(2)}, u32[]{:S(2)}) collective-permute-start(f32[128,128]{1,0:T(8,128)S(1)} %get-tuple-element.8), channel_id=1, source_target_pairs={{0,8},{8,16},{16,24},{24,0},{1,9},{9,17},{17,25},{25,1},{2,10},{10... | collective-permute-start | bytes 196616 | tf_op jit(solution)/shard_map/ppermute | solution.py:9
  31.4 8.6 %collective-permute-start.3 = (f32[128]{0:T(128)S(1)}, f32[128]{0:T(128)S(1)}, u32[]{:S(2)}, u32[]{:S(2)}) collective-permute-start(f32[128]{0:T(128)S(1)} %collective-permute-done), channel_id=1, source_target_pairs={{0,8},{8,16},{16,24},{24,0},{1,9},{9,17},{17,25},{25,1},{2,10},{10... | collective-permute-start | bytes 1544 | tf_op jit(solution)/shard_map/ppermute | solution.py:9
  32.8 7.3 %collective-permute-start.5 = (f32[128,64]{0,1:T(8,128)S(1)}, f32[128,64]{0,1:T(8,128)S(1)}, u32[]{:S(2)}, u32[]{:S(2)}) collective-permute-start(f32[128,64]{0,1:T(8,128)S(1)} %collective-permute-done.2), channel_id=1, source_target_pairs={{0,8},{8,16},{16,24},{24,0},{1,9},{9,17},{17,25},{25,1},{2,10},{10... | collective-permute-start | bytes 98312 | tf_op jit(solution)/shard_map/ppermute | solution.py:9
  34.3 5.2 %collective-permute-start.4 = (f32[128,128]{1,0:T(8,128)S(1)}, f32[128,128]{1,0:T(8,128)S(1)}, u32[]{:S(2)}, u32[]{:S(2)}) collective-permute-start(f32[128,128]{1,0:T(8,128)S(1)} %collective-permute-done.1), channel_id=1, source_target_pairs={{0,8},{8,16},{16,24},{24,0},{1,9},{9,17},{17,25},{25,1},{2,10},{10... | collective-permute-start | bytes 196616 | tf_op jit(solution)/shard_map/ppermute | solution.py:9
  55.9 1.4 copy-start.2
  56.5 4.0 %collective-permute-start.7 = (f32[128,64]{0,1:T(8,128)S(1)}, f32[128,64]{0,1:T(8,128)S(1)}, u32[]{:S(2)}, u32[]{:S(2)}) collective-permute-start(f32[128,64]{0,1:T(8,128)S(1)} %convolution_add_fusion.2), channel_id=1, source_target_pairs={{0,24},{8,0},{16,8},{24,16},{1,25},{9,1},{17,9},{25,17},{2,26},{10... | collective-permute-start | bytes 98312 | tf_op jit(solution)/shard_map/ppermute | solution.py:9
  123.9 0.8 copy-start.4
  124.6 0.9 copy-start.3
  125.7 54.3 %copy-start.1 = (f32[128,64]{0,1:T(8,128)}, f32[128,64]{0,1:T(8,128)S(1)}, u32[]{:S(2)}) copy-start(f32[128,64]{0,1:T(8,128)S(1)} %convolution_subtract_fusion) | copy-start | bytes 98308
Sparse Core Ops, SparseCore 0:
  41.8 30.1 reduce-scatter.1
where the time goes:
time: 188 us
  blocking collectives  109 us (58%)
  other arithmetic  25.3 us (13%)
  waiting for transfers between devices  16.1 us (9%)
  between operations  14.9 us (8%)
  starting transfers between devices  11.9 us (6%)
  matrix products  9.55 us (5%)
    psum x1, blocking collectives, on_device(): lax.psum(transposed(new_residual, new_residual), ('blk', 'inner'))  41.5 us
    psum x1, blocking collectives, on_device(): gram_raw, res_gram = lax.psum((local_gram, local_res), ('blk', 'inner'))  38.3 us
    all_gather x1, blocking collectives, on_device(): lax.all_gather(scaled, 'inner', axis=0, tiled=True)  15 us
    all_gather x1, blocking collectives, on_device(): lax.all_gather(direction, 'inner', axis=0, tiled=True)  14.3 us
    another operation x6, other arithmetic, chol_solve(): factor = jnp.linalg.cholesky(matrix)  13 us
    ppermute x8, starting transfers between devices, from_behind(): lax.ppermute(value, axis, [(i, (i + by) % size) for i in range(size)])  11.8 us
    reduce_scatter x1, waiting for transfers between devices, on_device(): lax.psum_scatter(partial_value, 'inner', scatter_dimension=0, tiled=True)  11.5 us
    another operation x4, other arithmetic, chol_solve(): return jax.scipy.linalg.cho_solve((factor, True), rhs_side)  11.1 us
  transfers between devices with their start and end apart: 9, of which 3 were waited for; matrix products, arithmetic and copies ran while one was open for 4% of the time, Pallas kernels for 0%

commit v1 on v0

v1 whole, which is shorter than its diff:
```python
import functools

import jax
import jax.numpy as jnp
from jax import lax
from jax.experimental import pallas as pl
from jax.experimental.pallas import tpu as pltpu
from jax.sharding import PartitionSpec as P

MESH = pl.DeviceIdType.MESH
HI = lax.Precision.HIGHEST


def mm(left, right, dims):
    return lax.dot_general(left, right, (dims, ((), ())), precision=HI, preferred_element_type=jnp.float32)


def nn(left, right):
    return mm(left, right, ((1,), (0,)))


def nt(left, right):
    return mm(left, right, ((1,), (1,)))


def tn(left, right):
    return mm(left, right, ((0,), (0,)))


def pack(value):
    half = value.shape[0] // 2
    return jnp.concatenate([value[:half], value[half:]], axis=1)


def unpack(value):
    half = value.shape[1] // 2
    return jnp.concatenate([value[:, :half], value[:, half:]], axis=0)


def eliminate(matrix, rhs_side):
    n = matrix.shape[0]
    work = jnp.concatenate([matrix, rhs_side], axis=1)
    rows = lax.broadcasted_iota(jnp.int32, work.shape, 0)
    for k in range(n):
        column = jnp.broadcast_to(work[:, k : k + 1], work.shape)
        pivot_row = work[k : k + 1, :] / column[k : k + 1, :]
        work = jnp.where(rows == k, pivot_row, work - column * pivot_row)
    return work[:, n:]


class Exchange:
    def __init__(self, src, slots, send, recv, me, n, device):
        self.src, self.slots, self.send, self.recv = src, slots, send, recv
        self.me, self.n, self.device = me, n, device

    def copy(self, offset, slot):
        return pltpu.make_async_remote_copy(
            src_ref=self.src,
            dst_ref=self.slots.at[slot],
            send_sem=self.send.at[offset],
            recv_sem=self.recv.at[slot],
            device_id=self.device(lax.rem(self.me + offset, self.n)),
            device_id_type=MESH,
        )

    def start(self, value):
        self.src[...] = value
        for offset in range(1, self.n):
            self.copy(offset, self.me).start()

    def finish(self):
        total = self.src[...]
        for offset in range(1, self.n):
            slot = lax.rem(self.me + self.n - offset, self.n)
            self.copy(offset, slot).wait_recv()
            total = total + self.slots[slot]
        for offset in range(1, self.n):
            self.copy(offset, self.me).wait_send()
        return total


def body(sizes, pts, scales, noise, iterate, residual, direction, out_i, out_r, out_d, *scratch):
    nb, nh, rows, rhs = sizes
    cbuf, c_send, c_recv, f_send, rbuf, r_send, r_recv, pout, pin, p_send, p_recv, dall = scratch[:12]
    rest = scratch[12:]
    b = lax.axis_index("blk")
    i = lax.axis_index("inner")
    core = lax.rem(i, 2)
    hi = i // 2
    sibling = {"inner": hi * 2 + 1 - core}

    def at_blk(place):
        return {"blk": place}

    def at_hi(place):
        return {"inner": place * 2 + core}

    def at_core(place):
        return {"inner": hi * 2 + place}

    ways = ((core, 2, at_core), (b, nb, at_blk), (hi, nh, at_hi))
    sums = []
    for which in range(3):
        stages = []
        for stage, (me, n, device) in enumerate(ways):
            src, slots, send, recv = rest[(which * 3 + stage) * 4 : (which * 3 + stage) * 4 + 4]
            stages.append(Exchange(src, slots, send, recv, me, n, device))
        sums.append(stages)
    sum_r, sum_a, sum_bc = sums

    barrier = pltpu.get_barrier_semaphore()
    for offset in range(1, nb):
        pl.semaphore_signal(barrier, inc=1, device_id=at_blk(lax.rem(b + offset, nb)), device_id_type=MESH)
    for offset in range(1, nh):
        pl.semaphore_signal(barrier, inc=1, device_id=at_hi(lax.rem(hi + offset, nh)), device_id_type=MESH)
    pl.semaphore_signal(barrier, inc=1, device_id=sibling, device_id_type=MESH)
    points = pts[...]
    rbuf[hi] = points
    cbuf[core, b, :rows] = points
    cbuf[core, b, rows:] = pack(direction[...])
    res = residual[...]
    own_res_gram = pack(tn(res, res))
    pl.semaphore_wait(barrier, nb + nh - 1)

    def c_copy(offset, slot):
        return pltpu.make_async_remote_copy(
            src_ref=cbuf.at[core, slot],
            dst_ref=cbuf.at[core, slot],
            send_sem=c_send.at[offset],
            recv_sem=c_recv.at[core, slot],
            device_id=at_blk(lax.rem(b + offset, nb)),
            device_id_type=MESH,
        )

    def f_copy(side, slot):
        return pltpu.make_async_remote_copy(
            src_ref=cbuf.at[side, slot],
            dst_ref=cbuf.at[side, slot],
            send_sem=f_send.at[slot],
            recv_sem=c_recv.at[side, slot],
            device_id=sibling,
            device_id_type=MESH,
        )

    def r_copy(offset, slot):
        return pltpu.make_async_remote_copy(
            src_ref=rbuf.at[slot],
            dst_ref=rbuf.at[slot],
            send_sem=r_send.at[offset],
            recv_sem=r_recv.at[slot],
            device_id=at_hi(lax.rem(hi + offset, nh)),
            device_id_type=MESH,
        )

    def p_copy(owner, slot):
        return pltpu.make_async_remote_copy(
            src_ref=pout.at[owner],
            dst_ref=pin.at[slot],
            send_sem=p_send.at[owner],
            recv_sem=p_recv.at[slot],
            device_id=at_hi(owner),
            device_id_type=MESH,
        )

    for offset in range(1, nh):
        r_copy(offset, hi).start()
    for offset in range(1, nb):
        c_copy(offset, b).start()
    f_copy(core, b).start()
    sum_r[0].start(own_res_gram)
    for offset in range(1, nb):
        slot = lax.rem(b + nb - offset, nb)
        c_copy(offset, slot).wait_recv()
        f_copy(core, slot).start()
    sum_r[1].start(sum_r[0].finish())
    for slot in range(nb):
        f_copy(1 - core, slot).wait_recv()

    scale = scales[...]
    for side in range(2):
        for slot in range(nb):
            block = pl.ds((side * nb + slot) * rows, rows)
            dall[block, :] = unpack(cbuf[side, slot, rows:])
    column_pts = jnp.concatenate(
        [cbuf[side, slot, :rows] / scale for side in range(2) for slot in range(nb)], axis=0
    )
    ones = jnp.ones((8, scale.shape[1]), jnp.float32)
    column_sq = 0.5 * nt(ones, column_pts * column_pts)[:1, :]

    def image_rows(place):
        left = rbuf[place] / scale
        left_sq = 0.5 * jnp.sum(left * left, axis=1, keepdims=True)
        tile = jnp.exp(nt(left, column_pts) - (left_sq + column_sq))
        return nn(tile, dall[...])

    image = image_rows(hi)
    for offset in range(1, nh):
        place = lax.rem(hi + nh - offset, nh)
        r_copy(offset, place).wait_recv()
        pout[place] = pack(image_rows(place))
        p_copy(place, hi).start()
    sum_r[2].start(sum_r[1].finish())
    res_gram = unpack(sum_r[2].finish())
    eye = lax.broadcasted_iota(jnp.int32, (rhs, rhs), 0) == lax.broadcasted_iota(jnp.int32, (rhs, rhs), 1)
    res_inverse = eliminate(res_gram, eye.astype(jnp.float32))

    direct = direction[...]
    image = image + noise[0, 0] * direct
    for offset in range(1, nh):
        place = lax.rem(hi + nh - offset, nh)
        p_copy(place, place).wait_recv()
        image = image + unpack(pin[place])
    own_gram = pack(0.5 * (tn(direct, image) + tn(image, direct)))
    sum_a[0].start(own_gram)
    sum_bc[0].start(tn(image, jnp.concatenate([res, image], axis=1)))
    sum_a[1].start(sum_a[0].finish())
    sum_bc[1].start(sum_bc[0].finish())
    sum_a[2].start(sum_a[1].finish())
    sum_bc[2].start(sum_bc[1].finish())
    gram = unpack(sum_a[2].finish())
    step = eliminate(gram, res_gram)
    both = sum_bc[2].finish()
    cross, square = both[:, :rhs], both[:, rhs:]
    moved = nn(square, step) - cross
    new_gram = res_gram + tn(
        jnp.concatenate([step, -cross], axis=0), jnp.concatenate([moved, step], axis=0)
    )
    correction = nn(res_inverse, new_gram)
    new_res = res - nn(image, step)
    out_i[...] = iterate[...] + nn(direct, step)
    out_r[...] = new_res
    out_d[...] = new_res + nn(direct, correction)

    for offset in range(1, nb):
        c_copy(offset, b).wait_send()
    for slot in range(nb):
        f_copy(core, slot).wait_send()
    for offset in range(1, nh):
        r_copy(offset, hi).wait_send()
        place = lax.rem(hi + nh - offset, nh)
        p_copy(place, hi).wait_send()


def solution(mesh):
    nb, ni = mesh.shape["blk"], mesh.shape["inner"]
    nh = ni // 2

    def on_device(points, lengthscales, noise_level, iterate, residual, direction):
        rows, features = points.shape
        rhs = direction.shape[1]
        f32, dma = jnp.float32, pltpu.SemaphoreType.DMA
        half = rows // 2
        scratch = [
            pltpu.VMEM((2, nb, rows + half, features), f32),
            dma((nb,)),
            dma((2, nb)),
            dma((nb,)),
            pltpu.VMEM((nh, rows, features), f32),
            dma((nh,)),
            dma((nh,)),
            pltpu.VMEM((nh, half, 2 * rhs), f32),
            pltpu.VMEM((nh, half, 2 * rhs), f32),
            dma((nh,)),
            dma((nh,)),
            pltpu.VMEM((2 * nb * rows, rhs), f32),
        ]
        for height in (rhs // 2, rhs // 2, rhs):
            for n in (2, nb, nh):
                scratch += [
                    pltpu.VMEM((height, 2 * rhs), f32),
                    pltpu.VMEM((n, height, 2 * rhs), f32),
                    dma((n,)),
                    dma((n,)),
                ]
        vmem = pl.BlockSpec(memory_space=pltpu.VMEM)
        out = jax.ShapeDtypeStruct((rows, rhs), f32)
        return pl.pallas_call(
            functools.partial(body, (nb, nh, rows, rhs)),
            out_shape=(out, out, out),
            in_specs=[vmem, vmem, pl.BlockSpec(memory_space=pltpu.SMEM), vmem, vmem, vmem],
            out_specs=(vmem, vmem, vmem),
            scratch_shapes=scratch,
            compiler_params=pltpu.CompilerParams(collective_id=0, has_side_effects=True),
            name="cg_step",
        )(points, lengthscales[None, :], noise_level[None, :], iterate, residual, direction)

    rows_spec = P(("blk", "inner"), None)
    return jax.shard_map(
        on_device,
        mesh=mesh,
        in_specs=(rows_spec, P(), P(), rows_spec, rows_spec, rows_spec),
        out_specs=(rows_spec, rows_spec, rows_spec),
        check_vma=False,
    )
```

time: 188 us -> 51.9 us (0.28)
  blocking collectives: 109 us -> 0 us
  Pallas kernels: 0 us -> 44.1 us
  other arithmetic: 25.3 us -> 0 us
  waiting for transfers between devices: 16.1 us -> 0 us
  between operations: 14.9 us -> 1.31 us
  starting transfers between devices: 11.9 us -> 0 us
  matrix products: 9.55 us -> 0 us
  local copies, waits for them, and re-layouts: 0.84 us -> 6.08 us
    psum x2 -> x0, blocking collectives: 79.8 us -> none  [the longest x1 41.5 us: on_device(): lax.psum(transposed(new_residual, new_residual), ('blk', 'inner'))]
    pallas_call x0 -> x1, Pallas kernels: none -> 44.1 us  [on_device(): pl.pallas_call(functools.partial(body, (nb, nh, rows, rhs)), out_shape=(o...]
    all_gather x2 -> x0, blocking collectives: 29.3 us -> none  [the longest x1 15 us: on_device(): lax.all_gather(scaled, 'inner', axis=0, tiled=True)]
    another operation x10 -> x0, other arithmetic: 24.1 us -> none  [the longest x6 13 us: chol_solve(): factor = jnp.linalg.cholesky(matrix)]
    ppermute x8 -> x0, starting transfers between devices: 11.8 us -> none  [from_behind(): lax.ppermute(value, axis, [(i, (i + by) % size) for i in range(size)])]
    reduce_scatter x1 -> x0, waiting for transfers between devices: 11.5 us -> none  [on_device(): lax.psum_scatter(partial_value, 'inner', scatter_dimension=0, tiled=True)]
    dot_general x13 -> x0, matrix products: 8.73 us -> none  [the longest x6 5.05 us: matmul(): jnp.dot(left, right, precision=lax.Precision.HIGHEST, preferred_element_t...]
    ppermute x8 -> x0, waiting for transfers between devices: 4.58 us -> none  [from_behind(): lax.ppermute(value, axis, [(i, (i + by) % size) for i in range(size)])]
  transfers between devices with their start and end apart: 9 -> 0, of which waited for: 3 -> 0; matrix products, arithmetic and copies ran while one was open for 4% -> 0% of each run, Pallas kernels for 0% -> 0%
where the time goes in v1:
time: 51.9 us; the launch traced here: 51.5 us
  Pallas kernels  44.1 us (85%)
  local copies, waits for them, and re-layouts  6.08 us (12%)
  between operations  1.31 us (3%)
    pallas_call x1, Pallas kernels, on_device(): pl.pallas_call(functools.partial(body, (nb, nh, rows, rhs)), out_shape=(o...  44.1 us
    unnamed x11, local copies, waits for them, and re-layouts  3.12 us
    pallas_call x3, local copies, waits for them, and re-layouts, on_device(): pl.pallas_call(functools.partial(body, (nb, nh, rows, rhs)), out_shape=(o...  2.96 us

profile of v1, /device:TPU:0, one launch (start us, length us, event | category | flops | bytes accessed | tf_op | source)
XLA Modules:
  0.0 51.5 jit_solution(8554154827284641606)
XLA Ops:
  1.3 0.0 copy-start.2
  1.3 1.5 %copy.9.iterate = f32[128,64]{1,0:T(8,128)} copy(f32[128,64]{0,1:T(8,128)} %param.9) | data formatting | bytes 65536 | tf_op args[3]
  2.8 0.0 copy-done.2
  2.8 0.0 copy-start.3
  2.8 0.7 %copy.10.residual = f32[128,64]{1,0:T(8,128)} copy(f32[128,64]{0,1:T(8,128)S(1)} %copy-done.2) | data formatting | bytes 65536 | tf_op args[4]
  3.5 0.0 copy-done.3
  3.5 0.7 %copy.11.direction = f32[128,64]{1,0:T(8,128)} copy(f32[128,64]{0,1:T(8,128)S(1)} %copy-done.3) | data formatting | bytes 65536 | tf_op args[5]
  4.3 44.1 %cg_step.1 = (f32[128,64]{1,0:T(8,128)}, f32[128,64]{1,0:T(8,128)}, f32[128,64]{1,0:T(8,128)}) custom-call(f32[128,128]{1,0:T(8,128)} %pts.1, f32[1,128]{1,0:T(1,128)} %bitcast.3, f32[1,1]{1,0:T(1,128)} %bitcast.2.noise, f32[128,64]{1,0:T(8,128)} %copy.9.iterate, f32[128,64]{1,0:T(8,128)} %copy.10.residual, f32[128,64]{1,0:T(8,128)} %copy.11.direction), custom_call_target="tpu_custom_call" | custom-call | tf_op jit(solution)/shard_map/cg_step/pallas_call | solution.py:277
  48.3 0.0 copy-start.1
  48.4 1.6 %copy.12 = f32[128,64]{0,1:T(8,128)} copy(f32[128,64]{1,0:T(8,128)} %get-tuple-element.3) | data formatting | bytes 65536 | tf_op jit(solution)/shard_map/cg_step/pallas_call | solution.py:277
  49.9 0.0 copy-done.1
  49.9 0.0 copy-start
  49.9 0.7 %copy.13 = f32[128,64]{0,1:T(8,128)} copy(f32[128,64]{1,0:T(8,128)S(1)} %copy-done.1) | data formatting | bytes 65536 | tf_op jit(solution)/shard_map/cg_step/pallas_call | solution.py:277
  50.6 0.1 copy-done
  50.8 0.7 %copy.14 = f32[128,64]{0,1:T(8,128)} copy(f32[128,64]{1,0:T(8,128)S(1)} %copy-done) | data formatting | bytes 65536 | tf_op jit(solution)/shard_map/cg_step/pallas_call | solution.py:277
Async XLA Ops:
  1.3 1.5 %copy-start.2 = (f32[128,64]{0,1:T(8,128)S(1)}, f32[128,64]{0,1:T(8,128)}, u32[]{:S(2)}) copy-start(f32[128,64]{0,1:T(8,128)} %param.10) | copy-start | bytes 98308
  2.8 0.8 %copy-start.3 = (f32[128,64]{0,1:T(8,128)S(1)}, f32[128,64]{0,1:T(8,128)}, u32[]{:S(2)}) copy-start(f32[128,64]{0,1:T(8,128)} %param.11) | copy-start | bytes 98308
  48.3 1.6 %copy-start.1 = (f32[128,64]{1,0:T(8,128)S(1)}, f32[128,64]{1,0:T(8,128)}, u32[]{:S(2)}) copy-start(f32[128,64]{1,0:T(8,128)} %get-tuple-element.4) | copy-start | bytes 98308
  49.9 0.8 %copy-start = (f32[128,64]{1,0:T(8,128)S(1)}, f32[128,64]{1,0:T(8,128)}, u32[]{:S(2)}) copy-start(f32[128,64]{1,0:T(8,128)} %get-tuple-element.5) | copy-start | bytes 98308

commit v2 on v1

v2 whole, which is shorter than its diff:
```python
import functools

import jax
import jax.numpy as jnp
from jax import lax
from jax.experimental import pallas as pl
from jax.experimental.pallas import tpu as pltpu
from jax.sharding import PartitionSpec as P

MESH = pl.DeviceIdType.MESH
HI = lax.Precision.HIGHEST


def mm(left, right, dims):
    return lax.dot_general(left, right, (dims, ((), ())), precision=HI, preferred_element_type=jnp.float32)


def nn(left, right):
    return mm(left, right, ((1,), (0,)))


def nt(left, right):
    return mm(left, right, ((1,), (1,)))


def tn(left, right):
    return mm(left, right, ((0,), (0,)))


def pack(value):
    half = value.shape[0] // 2
    return jnp.concatenate([value[:half], value[half:]], axis=1)


def unpack(value):
    half = value.shape[1] // 2
    return jnp.concatenate([value[:, :half], value[:, half:]], axis=0)


def partner(me, offset, n):
    if n & (n - 1):
        return lax.rem(me + offset, n)
    place, bit = me, 1
    while bit < n:
        if offset & bit:
            place = place + bit - 2 * bit * lax.rem(me // bit, 2)
        bit *= 2
    return place


def source(me, offset, n):
    if n & (n - 1):
        return lax.rem(me + n - offset, n)
    return partner(me, offset, n)


def eliminate(matrix, rhs_side):
    n = matrix.shape[0]
    work = jnp.concatenate([matrix, rhs_side], axis=1)
    rows = lax.broadcasted_iota(jnp.int32, work.shape, 0)
    for k in range(0, n, 2):
        column0 = jnp.broadcast_to(work[:, k : k + 1], work.shape)
        column1 = jnp.broadcast_to(work[:, k + 1 : k + 2], work.shape)
        row0, row1 = work[k : k + 1], work[k + 1 : k + 2]
        upper = column1[k : k + 1]
        inverse = 1.0 / column0[k : k + 1]
        lower = column0[k + 1 : k + 2] * inverse
        second = (row1 - lower * row0) / (column1[k + 1 : k + 2] - lower * upper)
        first = (row0 - upper * second) * inverse
        below = work - column0 * first - column1 * second
        work = jnp.where(rows == k, first, jnp.where(rows == k + 1, second, below))
    return work[:, n:]


class Exchange:
    def __init__(self, src, slots, send, recv, me, n, device):
        self.src, self.slots, self.send, self.recv = src, slots, send, recv
        self.me, self.n, self.device = me, n, device

    def copy(self, offset, slot):
        return pltpu.make_async_remote_copy(
            src_ref=self.src,
            dst_ref=self.slots.at[slot],
            send_sem=self.send.at[offset],
            recv_sem=self.recv.at[slot],
            device_id=self.device(partner(self.me, offset, self.n)),
            device_id_type=MESH,
        )

    def start(self, value):
        self.src[...] = value
        for offset in range(1, self.n):
            self.copy(offset, self.me).start()

    def finish(self):
        total = self.src[...]
        for offset in range(1, self.n):
            slot = source(self.me, offset, self.n)
            self.copy(offset, slot).wait_recv()
            total = total + self.slots[slot]
        for offset in range(1, self.n):
            self.copy(offset, self.me).wait_send()
        return total


def body(sizes, pts, scales, noise, iterate, residual, direction, out_i, out_r, out_d, *scratch):
    nb, nh, rows, rhs = sizes
    cbuf, c_send, c_recv, f_send, rbuf, r_send, r_recv = scratch[:7]
    dbuf, d_send, d_recv, pout, pin, p_send, p_recv = scratch[7:14]
    rest = scratch[14:]
    b = lax.axis_index("blk")
    i = lax.axis_index("inner")
    core = lax.rem(i, 2)
    hi = i // 2
    sibling = {"inner": hi * 2 + 1 - core}

    def at_blk(place):
        return {"blk": place}

    def at_hi(place):
        return {"inner": place * 2 + core}

    def at_core(place):
        return {"inner": hi * 2 + place}

    ways = ((core, 2, at_core), (b, nb, at_blk), (hi, nh, at_hi))
    sums = []
    for which in range(3):
        stages = []
        for stage, (me, n, device) in enumerate(ways):
            src, slots, send, recv = rest[(which * 3 + stage) * 4 : (which * 3 + stage) * 4 + 4]
            stages.append(Exchange(src, slots, send, recv, me, n, device))
        sums.append(stages)
    sum_r, sum_a, sum_bc = sums

    barrier = pltpu.get_barrier_semaphore()
    for offset in range(1, nb):
        pl.semaphore_signal(barrier, inc=1, device_id=at_blk(partner(b, offset, nb)), device_id_type=MESH)
    for offset in range(1, nh):
        pl.semaphore_signal(barrier, inc=1, device_id=at_hi(partner(hi, offset, nh)), device_id_type=MESH)
    pl.semaphore_signal(barrier, inc=1, device_id=sibling, device_id_type=MESH)
    cbuf[core, b, :rows] = pts[...]
    cbuf[core, b, rows:] = direction[...]
    res = residual[...]
    direct = direction[...]
    own_res_gram = pack(nt(res, res))
    pl.semaphore_wait(barrier, nb + nh - 1)

    def c_copy(offset, slot):
        return pltpu.make_async_remote_copy(
            src_ref=cbuf.at[core, slot],
            dst_ref=cbuf.at[core, slot],
            send_sem=c_send.at[offset],
            recv_sem=c_recv.at[core, slot],
            device_id=at_blk(partner(b, offset, nb)),
            device_id_type=MESH,
        )

    def f_copy(side, slot):
        return pltpu.make_async_remote_copy(
            src_ref=cbuf.at[side, slot],
            dst_ref=cbuf.at[side, slot],
            send_sem=f_send.at[slot],
            recv_sem=c_recv.at[side, slot],
            device_id=sibling,
            device_id_type=MESH,
        )

    def r_copy(offset, slot):
        return pltpu.make_async_remote_copy(
            src_ref=pts,
            dst_ref=rbuf.at[slot],
            send_sem=r_send.at[offset],
            recv_sem=r_recv.at[slot],
            device_id=at_hi(partner(hi, offset, nh)),
            device_id_type=MESH,
        )

    def d_copy(offset, slot):
        return pltpu.make_async_remote_copy(
            src_ref=direction,
            dst_ref=dbuf.at[slot],
            send_sem=d_send.at[offset],
            recv_sem=d_recv.at[slot],
            device_id=at_hi(partner(hi, offset, nh)),
            device_id_type=MESH,
        )

    def p_copy(owner, slot):
        return pltpu.make_async_remote_copy(
            src_ref=pout.at[owner],
            dst_ref=pin.at[slot],
            send_sem=p_send.at[owner],
            recv_sem=p_recv.at[slot],
            device_id=at_hi(owner),
            device_id_type=MESH,
        )

    for offset in range(1, nb):
        c_copy(offset, b).start()
    for offset in range(1, nh):
        r_copy(offset, hi).start()
    f_copy(core, b).start()
    sum_r[0].start(own_res_gram)
    for offset in range(1, nh):
        d_copy(offset, hi).start()
    sum_r[1].start(sum_r[0].finish())
    for offset in range(1, nb):
        slot = source(b, offset, nb)
        c_copy(offset, slot).wait_recv()
        f_copy(core, slot).start()
    sum_r[2].start(sum_r[1].finish())
    for slot in range(nb):
        f_copy(1 - core, slot).wait_recv()

    scale = scales[...]
    blocks = [(side, slot) for side in range(2) for slot in range(nb)]
    directions = jnp.concatenate([cbuf[side, slot, rows:] for side, slot in blocks], axis=1)
    column_pts = jnp.concatenate([cbuf[side, slot, :rows] / scale for side, slot in blocks], axis=0)
    column_sq = 0.5 * jnp.sum(column_pts * column_pts, axis=1, keepdims=True)
    ones = jnp.ones((8, scale.shape[1]), jnp.float32)

    def image_part(block):
        left = block / scale
        left_sq = 0.5 * nt(ones, left * left)[:1, :]
        tile = jnp.exp(nt(column_pts, left) - (column_sq + left_sq))
        return nn(directions, tile)

    image = image_part(pts[...]) + noise[0, 0] * direct
    parts, others = [image], [direct]
    for offset in range(1, nh):
        place = source(hi, offset, nh)
        r_copy(offset, place).wait_recv()
        part = image_part(rbuf[place])
        pout[place] = part
        p_copy(place, hi).start()
        parts.append(part)
    for offset in range(1, nh):
        place = source(hi, offset, nh)
        d_copy(offset, place).wait_recv()
        others.append(dbuf[place])
    own_gram = 0.5 * nt(jnp.concatenate(others + parts, axis=1), jnp.concatenate(parts + others, axis=1))
    sum_a[0].start(pack(own_gram))
    sum_a[1].start(sum_a[0].finish())

    res_gram = unpack(sum_r[2].finish())
    eye = lax.broadcasted_iota(jnp.int32, (rhs, rhs), 0) == lax.broadcasted_iota(jnp.int32, (rhs, rhs), 1)
    res_inverse = eliminate(res_gram, eye.astype(jnp.float32))

    sum_a[2].start(sum_a[1].finish())
    for offset in range(1, nh):
        place = source(hi, offset, nh)
        p_copy(place, place).wait_recv()
        image = image + pin[place]
    sum_bc[0].start(nt(image, jnp.concatenate([res, image], axis=0)))
    sum_bc[1].start(sum_bc[0].finish())
    sum_bc[2].start(sum_bc[1].finish())
    gram = unpack(sum_a[2].finish())
    step = eliminate(gram, res_gram)
    new_res = res - tn(step, image)
    out_i[...] = iterate[...] + tn(step, direct)
    out_r[...] = new_res
    both = sum_bc[2].finish()
    cross, square = both[:, :rhs], both[:, rhs:]
    moved = nn(square, step) - cross
    new_gram = res_gram + tn(
        jnp.concatenate([step, -cross], axis=0), jnp.concatenate([moved, step], axis=0)
    )
    correction = nn(res_inverse, new_gram)
    out_d[...] = new_res + tn(correction, direct)

    for offset in range(1, nb):
        c_copy(offset, b).wait_send()
    for slot in range(nb):
        f_copy(core, slot).wait_send()
    for offset in range(1, nh):
        r_copy(offset, hi).wait_send()
        d_copy(offset, hi).wait_send()
        p_copy(source(hi, offset, nh), hi).wait_send()


def solution(mesh):
    nb, ni = mesh.shape["blk"], mesh.shape["inner"]
    nh = ni // 2

    def on_device(points, lengthscales, noise_level, iterate, residual, direction):
        rows, features = points.shape
        rhs = direction.shape[1]
        f32, dma = jnp.float32, pltpu.SemaphoreType.DMA
        scratch = [
            pltpu.VMEM((2, nb, rows + rhs, features), f32),
            dma((nb,)),
            dma((2, nb)),
            dma((nb,)),
            pltpu.VMEM((nh, rows, features), f32),
            dma((nh,)),
            dma((nh,)),
            pltpu.VMEM((nh, rhs, rows), f32),
            dma((nh,)),
            dma((nh,)),
            pltpu.VMEM((nh, rhs, rows), f32),
            pltpu.VMEM((nh, rhs, rows), f32),
            dma((nh,)),
            dma((nh,)),
        ]
        for height in (rhs // 2, rhs // 2, rhs):
            for n in (2, nb, nh):
                scratch += [
                    pltpu.VMEM((height, 2 * rhs), f32),
                    pltpu.VMEM((n, height, 2 * rhs), f32),
                    dma((n,)),
                    dma((n,)),
                ]
        vmem = pl.BlockSpec(memory_space=pltpu.VMEM)
        out = jax.ShapeDtypeStruct((rhs, rows), f32)
        results = pl.pallas_call(
            functools.partial(body, (nb, nh, rows, rhs)),
            out_shape=(out, out, out),
            in_specs=[vmem, vmem, pl.BlockSpec(memory_space=pltpu.SMEM), vmem, vmem, vmem],
            out_specs=(vmem, vmem, vmem),
            scratch_shapes=scratch,
            compiler_params=pltpu.CompilerParams(collective_id=0, has_side_effects=True),
            name="cg_step",
        )(points, lengthscales[None, :], noise_level[None, :], iterate.T, residual.T, direction.T)
        return tuple(result.T for result in results)

    rows_spec = P(("blk", "inner"), None)
    return jax.shard_map(
        on_device,
        mesh=mesh,
        in_specs=(rows_spec, P(), P(), rows_spec, rows_spec, rows_spec),
        out_specs=(rows_spec, rows_spec, rows_spec),
        check_vma=False,
    )
```

time: 51.9 us -> 42.4 us (0.82)
  Pallas kernels: 44.1 us -> 38.1 us
  local copies, waits for them, and re-layouts: 6.08 us -> 2.77 us
    pallas_call x1, Pallas kernels: 44.1 us -> 38.1 us  [on_device(): pl.pallas_call(functools.partial(body, (nb, nh, rows, rhs)), out_shape=(o...]
    pallas_call x3 -> x0, local copies, waits for them, and re-layouts: 2.96 us -> none  [on_device(): pl.pallas_call(functools.partial(body, (nb, nh, rows, rhs)), out_shape=(o...]
    unnamed x11 -> x7, local copies, waits for them, and re-layouts: 3.12 us -> 2.77 us
where the time goes in v2:
time: 42.4 us; the launch traced here: 42.1 us
  Pallas kernels  38.1 us (90%)
  local copies, waits for them, and re-layouts  2.77 us (7%)
  between operations  1.3 us (3%)
    pallas_call x1, Pallas kernels, on_device(): pl.pallas_call(functools.partial(body, (nb, nh, rows, rhs)), out_shape=(o...  38.1 us
    unnamed x7, local copies, waits for them, and re-layouts  2.77 us

profile of v2, /device:TPU:0, one launch (start us, length us, event | category | flops | bytes accessed | tf_op | source)
XLA Modules:
  0.0 42.1 jit_solution(8277454695654163753)
XLA Ops:
  1.3 38.1 %cg_step.1 = (f32[64,128]{1,0:T(8,128)}, f32[64,128]{1,0:T(8,128)}, f32[64,128]{1,0:T(8,128)}) custom-call(f32[128,128]{1,0:T(8,128)} %pts.1, f32[1,128]{1,0:T(1,128)} %bitcast.15, f32[1,1]{1,0:T(1,128)} %bitcast.8.noise, f32[64,128]{1,0:T(8,128)} %bitcast.9, f32[64,128]{1,0:T(8,128)} %bitcast.10, f32[64,128]{1,0:T(8,128)} %bitcast.11), custom_call_target="tpu_custom_call" | custom-call | tf_op jit(solution)/shard_map/cg_step/pallas_call | solution.py:316
  39.4 0.0 copy-start.1
  39.4 1.4 %copy.13 = f32[128,64]{0,1:T(8,128)} copy(f32[128,64]{0,1:T(8,128)} %bitcast.14) | data formatting | bytes 65536
  40.7 0.0 copy-done.1
  40.7 0.0 copy-start
  40.7 0.6 %copy.14 = f32[128,64]{0,1:T(8,128)} copy(f32[128,64]{0,1:T(8,128)S(1)} %bitcast.13) | data formatting | bytes 65536
  41.4 0.2 copy-done
  41.5 0.6 %copy.15 = f32[128,64]{0,1:T(8,128)} copy(f32[128,64]{0,1:T(8,128)S(1)} %bitcast.12) | data formatting | bytes 65536
Async XLA Ops:
  39.4 1.4 %copy-start.1 = (f32[64,128]{1,0:T(8,128)S(1)}, f32[64,128]{1,0:T(8,128)}, u32[]{:S(2)}) copy-start(f32[64,128]{1,0:T(8,128)} %get-tuple-element.7) | copy-start | bytes 98308
  40.7 0.8 %copy-start = (f32[64,128]{1,0:T(8,128)S(1)}, f32[64,128]{1,0:T(8,128)}, u32[]{:S(2)}) copy-start(f32[64,128]{1,0:T(8,128)} %get-tuple-element.8) | copy-start | bytes 98308

commit v3 on v2

--- a/solution.py
+++ b/solution.py
@@ -103,7 +103,7 @@
         return total
 
 
-def body(sizes, pts, scales, noise, iterate, residual, direction, out_i, out_r, out_d, *scratch):
+def body(sizes, pts, scales, noise, iterate, residual, direction, out, *scratch):
     nb, nh, rows, rhs = sizes
     cbuf, c_send, c_recv, f_send, rbuf, r_send, r_recv = scratch[:7]
     dbuf, d_send, d_recv, pout, pin, p_send, p_recv = scratch[7:14]
@@ -205,36 +205,59 @@
     for offset in range(1, nh):
         d_copy(offset, hi).start()
     sum_r[1].start(sum_r[0].finish())
-    for offset in range(1, nb):
-        slot = source(b, offset, nb)
-        c_copy(offset, slot).wait_recv()
-        f_copy(core, slot).start()
+    scale = scales[...]
+    ones = jnp.ones((8, scale.shape[1]), jnp.float32)
+    places = [hi] + [source(hi, offset, nh) for offset in range(1, nh)]
+    slots = [b] + [source(b, offset, nb) for offset in range(1, nb)]
+
+    def row_group(first):
+        members = range(first, min(first + 2, nh))
+        for member in members:
+            if member > 0:
+                r_copy(member, places[member]).wait_recv()
+        raw = [pts[...] if member == 0 else rbuf[places[member]] for member in members]
+        left = jnp.concatenate(raw, axis=0) / scale
+        return left, 0.5 * nt(ones, left * left)[:1, :]
+
+    def column_set(members):
+        blocks = [(side, slots[member]) for member in members for side in (core, 1 - core)]
+        right = jnp.concatenate([cbuf[side, slot, :rows] / scale for side, slot in blocks], axis=0)
+        right_sq = 0.5 * jnp.sum(right * right, axis=1, keepdims=True)
+        return right, right_sq, jnp.concatenate([cbuf[side, slot, rows:] for side, slot in blocks], axis=1)
+
+    def image_part(group, columns):
+        left, left_sq = group
+        right, right_sq, directions = columns
+        return nn(directions, jnp.exp(nt(right, left) - (right_sq + left_sq)))
+
+    def forward(offset):
+        c_copy(offset, slots[offset]).wait_recv()
+        f_copy(core, slots[offset]).start()
+
+    last = nb - 1
+    for offset in range(1, last):
+        forward(offset)
+    for offset in range(last):
+        f_copy(1 - core, slots[offset]).wait_recv()
+    group = row_group(0)
+    early = column_set(range(last))
+    images = image_part(group, early)
+    forward(last)
     sum_r[2].start(sum_r[1].finish())
-    for slot in range(nb):
-        f_copy(1 - core, slot).wait_recv()
-
-    scale = scales[...]
-    blocks = [(side, slot) for side in range(2) for slot in range(nb)]
-    directions = jnp.concatenate([cbuf[side, slot, rows:] for side, slot in blocks], axis=1)
-    column_pts = jnp.concatenate([cbuf[side, slot, :rows] / scale for side, slot in blocks], axis=0)
-    column_sq = 0.5 * jnp.sum(column_pts * column_pts, axis=1, keepdims=True)
-    ones = jnp.ones((8, scale.shape[1]), jnp.float32)
-
-    def image_part(block):
-        left = block / scale
-        left_sq = 0.5 * nt(ones, left * left)[:1, :]
-        tile = jnp.exp(nt(column_pts, left) - (column_sq + left_sq))
-        return nn(directions, tile)
-
-    image = image_part(pts[...]) + noise[0, 0] * direct
-    parts, others = [image], [direct]
-    for offset in range(1, nh):
-        place = source(hi, offset, nh)
-        r_copy(offset, place).wait_recv()
-        part = image_part(rbuf[place])
-        pout[place] = part
-        p_copy(place, hi).start()
-        parts.append(part)
+    f_copy(1 - core, slots[last]).wait_recv()
+    late = column_set([last])
+    images = images + image_part(group, late)
+    parts = [images[:, :rows] + noise[0, 0] * direct]
+    everything = tuple(jnp.concatenate(pair, axis=axis) for pair, axis in zip(zip(early, late), (0, 0, 1)))
+    for first in range(0, nh, 2):
+        if first > 0:
+            images = image_part(row_group(first), everything)
+        for member in range(max(first, 1), min(first + 2, nh)):
+            part = images[:, (member - first) * rows : (member - first + 1) * rows]
+            pout[places[member]] = part
+            p_copy(places[member], hi).start()
+            parts.append(part)
+    image, others = parts[0], [direct]
     for offset in range(1, nh):
         place = source(hi, offset, nh)
         d_copy(offset, place).wait_recv()
@@ -258,8 +281,8 @@
     gram = unpack(sum_a[2].finish())
     step = eliminate(gram, res_gram)
     new_res = res - tn(step, image)
-    out_i[...] = iterate[...] + tn(step, direct)
-    out_r[...] = new_res
+    out[0] = iterate[...] + tn(step, direct)
+    out[1] = new_res
     both = sum_bc[2].finish()
     cross, square = both[:, :rhs], both[:, rhs:]
     moved = nn(square, step) - cross
@@ -267,7 +290,7 @@
         jnp.concatenate([step, -cross], axis=0), jnp.concatenate([moved, step], axis=0)
     )
     correction = nn(res_inverse, new_gram)
-    out_d[...] = new_res + tn(correction, direct)
+    out[2] = new_res + tn(correction, direct)
 
     for offset in range(1, nb):
         c_copy(offset, b).wait_send()
@@ -277,6 +300,11 @@
         r_copy(offset, hi).wait_send()
         d_copy(offset, hi).wait_send()
         p_copy(source(hi, offset, nh), hi).wait_send()
+
+
+def split(stacked, out_i, out_r, out_d):
+    for place, out in enumerate((out_i, out_r, out_d)):
+        out[...] = stacked[place]
 
 
 def solution(mesh):
@@ -313,15 +341,18 @@
                 ]
         vmem = pl.BlockSpec(memory_space=pltpu.VMEM)
         out = jax.ShapeDtypeStruct((rhs, rows), f32)
-        results = pl.pallas_call(
+        stacked = pl.pallas_call(
             functools.partial(body, (nb, nh, rows, rhs)),
-            out_shape=(out, out, out),
+            out_shape=jax.ShapeDtypeStruct((3, rhs, rows), f32),
             in_specs=[vmem, vmem, pl.BlockSpec(memory_space=pltpu.SMEM), vmem, vmem, vmem],
-            out_specs=(vmem, vmem, vmem),
+            out_specs=vmem,
             scratch_shapes=scratch,
             compiler_params=pltpu.CompilerParams(collective_id=0, has_side_effects=True),
             name="cg_step",
         )(points, lengthscales[None, :], noise_level[None, :], iterate.T, residual.T, direction.T)
+        results = pl.pallas_call(
+            split, out_shape=(out, out, out), in_specs=[vmem], out_specs=(vmem, vmem, vmem), name="split"
+        )(stacked)
         return tuple(result.T for result in results)
 
     rows_spec = P(("blk", "inner"), None)

time: 42.4 us -> 40 us (0.943)
  local copies, waits for them, and re-layouts: 2.77 us -> 0 us
    unnamed x7 -> x0, local copies, waits for them, and re-layouts: 2.77 us -> none
    pallas_call x1 -> x2, Pallas kernels: 38.1 us -> 38.5 us  [the longest x1 37 us: on_device(): pl.pallas_call(functools.partial(body, (nb, nh, rows, rhs)), out_shape=ja...]
where the time goes in v3:
time: 40 us; the launch traced here: 39.8 us
  Pallas kernels  38.5 us (96%)
  between operations  1.28 us (3%)
    pallas_call x1, Pallas kernels, on_device(): pl.pallas_call(functools.partial(body, (nb, nh, rows, rhs)), out_shape=ja...  37 us
    pallas_call x1, Pallas kernels, on_device(): pl.pallas_call(split, out_shape=(out, out, out), in_specs=[vmem], out_spe...  1.53 us

profile of v3, /device:TPU:0, one launch (start us, length us, event | category | flops | bytes accessed | tf_op | source)
XLA Modules:
  0.0 39.8 jit_solution(15676360521392739168)
XLA Ops:
  1.3 37.0 %cg_step.1.stacked = f32[3,64,128]{2,1,0:T(8,128)} custom-call(f32[128,128]{1,0:T(8,128)} %pts.1, f32[1,128]{1,0:T(1,128)} %bitcast.12, f32[1,1]{1,0:T(1,128)} %bitcast.8.noise, f32[64,128]{1,0:T(8,128)} %bitcast.9, f32[64,128]{1,0:T(8,128)} %bitcast.10, f32[64,128]{1,0:T(8,128)} %bitcast.11), custom_call_target="tpu_custom_call" | custom-call | tf_op jit(solution)/shard_map/cg_step/pallas_call | solution.py:344
  38.3 1.5 %split.1 = (f32[64,128]{1,0:T(8,128)}, f32[64,128]{1,0:T(8,128)}, f32[64,128]{1,0:T(8,128)}) custom-call(f32[3,64,128]{2,1,0:T(8,128)} %cg_step.1.stacked), custom_call_target="tpu_custom_call" | custom-call | tf_op jit(solution)/shard_map/split/pallas_call | solution.py:353

commit v4 on v3

--- a/solution.py
+++ b/solution.py
@@ -266,30 +266,30 @@
     sum_a[0].start(pack(own_gram))
     sum_a[1].start(sum_a[0].finish())
 
-    res_gram = unpack(sum_r[2].finish())
-    eye = lax.broadcasted_iota(jnp.int32, (rhs, rhs), 0) == lax.broadcasted_iota(jnp.int32, (rhs, rhs), 1)
-    res_inverse = eliminate(res_gram, eye.astype(jnp.float32))
-
-    sum_a[2].start(sum_a[1].finish())
     for offset in range(1, nh):
         place = source(hi, offset, nh)
         p_copy(place, place).wait_recv()
         image = image + pin[place]
     sum_bc[0].start(nt(image, jnp.concatenate([res, image], axis=0)))
+    sum_a[2].start(sum_a[1].finish())
     sum_bc[1].start(sum_bc[0].finish())
+    res_gram = unpack(sum_r[2].finish())
+    unit = lax.broadcasted_iota(jnp.int32, (rhs, rhs), 0) == lax.broadcasted_iota(jnp.int32, (rhs, rhs), 1)
+    unit = unit.astype(jnp.float32)
+    res_inverse = eliminate(res_gram, unit)
     sum_bc[2].start(sum_bc[1].finish())
     gram = unpack(sum_a[2].finish())
     step = eliminate(gram, res_gram)
     new_res = res - tn(step, image)
     out[0] = iterate[...] + tn(step, direct)
     out[1] = new_res
+    ahead = nt(res_inverse, step)
     both = sum_bc[2].finish()
     cross, square = both[:, :rhs], both[:, rhs:]
-    moved = nn(square, step) - cross
-    new_gram = res_gram + tn(
-        jnp.concatenate([step, -cross], axis=0), jnp.concatenate([moved, step], axis=0)
+    turned = nt(res_inverse, cross)
+    correction = unit - nn(ahead, cross) + nn(
+        jnp.concatenate([ahead, -turned], axis=1), jnp.concatenate([nn(square, step), step], axis=0)
     )
-    correction = nn(res_inverse, new_gram)
     out[2] = new_res + tn(correction, direct)
 
     for offset in range(1, nb):

time: 40 us -> 39.4 us (0.985)
  Pallas kernels: 38.5 us -> 37.9 us
    pallas_call x1, Pallas kernels: 37 us -> 36.4 us  [on_device(): pl.pallas_call(functools.partial(body, (nb, nh, rows, rhs)), out_shape=ja...]
where the time goes in v4:
time: 39.4 us; the launch traced here: 39.2 us
  Pallas kernels  37.9 us (96%)
  between operations  1.28 us (3%)
    pallas_call x1, Pallas kernels, on_device(): pl.pallas_call(functools.partial(body, (nb, nh, rows, rhs)), out_shape=ja...  36.4 us
    pallas_call x1, Pallas kernels, on_device(): pl.pallas_call(split, out_shape=(out, out, out), in_specs=[vmem], out_spe...  1.53 us

profile of v4, /device:TPU:0, one launch (start us, length us, event | category | flops | bytes accessed | tf_op | source)
XLA Modules:
  0.0 39.2 jit_solution(15280689064143079056)
XLA Ops:
  1.3 36.4 %cg_step.1.stacked = f32[3,64,128]{2,1,0:T(8,128)} custom-call(f32[128,128]{1,0:T(8,128)} %pts.1, f32[1,128]{1,0:T(1,128)} %bitcast.12, f32[1,1]{1,0:T(1,128)} %bitcast.8.noise, f32[64,128]{1,0:T(8,128)} %bitcast.9, f32[64,128]{1,0:T(8,128)} %bitcast.10, f32[64,128]{1,0:T(8,128)} %bitcast.11), custom_call_target="tpu_custom_call" | custom-call | tf_op jit(solution)/shard_map/cg_step/pallas_call | solution.py:344
  37.7 1.5 %split.1 = (f32[64,128]{1,0:T(8,128)}, f32[64,128]{1,0:T(8,128)}, f32[64,128]{1,0:T(8,128)}) custom-call(f32[3,64,128]{2,1,0:T(8,128)} %cg_step.1.stacked), custom_call_target="tpu_custom_call" | custom-call | tf_op jit(solution)/shard_map/split/pallas_call | solution.py:353
